TPU v7x, 32 devices: a whole 2x2x4 slice. The times are simulated.
32 devices in a mesh: level: 8 (over z, y), bal: 4 (over x, core).
Axes of the slice: x: 2, y: 2, z: 4, core: 2. Of those that a mesh axis runs over, the one named last changes fastest.
Arguments:
- patches: float32 [640, 5, 4096], P(('level', 'bal')), may hold values from -6 to 6
- patch_ids: int32 [640], P(('level', 'bal')), may hold values from 0 to 639, each once
- live: int32 [32], P(('level', 'bal')), may hold values from 4 to 12, as said below
- counts: int32 [2, 32], P(None, ('level', 'bal')), may hold values from 0 to 4, as said below
- parent_of: int32 [640], replicated, may hold values from 0 to 15
Outputs:
- new_patches: float32 [640, 5, 4096], P(('level', 'bal'))
- new_ids: int32 [640], P(('level', 'bal'))
- coarse: float32 [16, 5, 512], P('level')
Inputs may be any that keep to these rules, and one draw needn't show every extreme that they name: In every level group one device holds exactly 12 live patches. counts[r, d] never exceeds the live patches of device d at the start of round r; in every round and level group some device sends exactly 4.
All inputs are finite; a program needn't handle non-finite values.
Results may differ from a plain program's by a relative error of at most 0.0003.
Values sent between devices are 32-bit elements; how exact they have to be, the bound alone decides.
A program may use at most 64 MiB of HBM per device.

v0:
```python
import jax
import jax.numpy as jnp
from jax import lax
from jax.sharding import PartitionSpec as P

EDGE = 16
VARS = 5
SEND_MOST = 4
PAR_DEV = 2


def from_partner(array, axis, stride):
    return lax.ppermute(array, axis, [(i, i ^ 1 << stride) for i in range(lax.axis_size(axis))])


def restrict(fine_rows):
    leading = fine_rows.shape[:-1]
    half_edge = EDGE // 2
    blocks = fine_rows.reshape(leading + (half_edge, 2, half_edge, 2, half_edge, 2))
    return jnp.mean(blocks, axis=(-5, -3, -1)).reshape(
        leading + (half_edge * half_edge * half_edge,)
    )


def take_top(fine_rows, fine_ids, held_count, sent_count):
    capacity = fine_rows.shape[0]
    lane_index = jnp.arange(SEND_MOST, dtype=jnp.int32)
    pick_index = jnp.clip(held_count - sent_count + lane_index, 0, capacity - 1)
    is_valid = lane_index < sent_count
    return (
        jnp.where(is_valid[:, None, None], fine_rows[pick_index], 0.0),
        jnp.where(is_valid, fine_ids[pick_index], -1),
    )


def place_rows(fine_rows, fine_ids, kept_count, in_rows, in_ids):
    capacity = fine_rows.shape[0]
    slot_index = jnp.arange(capacity, dtype=jnp.int32)
    offset = slot_index - kept_count
    is_hit = (offset >= 0) & (offset < SEND_MOST)
    place_index = jnp.clip(offset, 0, SEND_MOST - 1)
    is_kept = slot_index < kept_count
    new_rows = jnp.where(
        is_kept[:, None, None],
        fine_rows,
        jnp.where(is_hit[:, None, None], in_rows[place_index], 0.0),
    )
    new_ids = jnp.where(is_kept, fine_ids, jnp.where(is_hit, in_ids[place_index], -1))
    return (new_rows, new_ids)


def pairwise_move(fine_rows, fine_ids, held_count, counts, rounds):
    for turn_index in range(rounds):
        sent_count = counts[turn_index, 0]
        out_rows, out_ids = take_top(fine_rows, fine_ids, held_count, sent_count)
        in_rows, in_marks = from_partner((out_rows, out_ids.astype(jnp.float32)), "bal", turn_index)
        in_ids = in_marks.astype(jnp.int32)
        kept_count = held_count - sent_count
        fine_rows, fine_ids = place_rows(fine_rows, fine_ids, kept_count, in_rows, in_ids)
        held_count = kept_count + jnp.sum((in_ids >= 0).astype(jnp.int32))
    return (fine_rows, fine_ids)


def parent_sums(fine_rows, fine_ids, parent_of):
    capacity = fine_rows.shape[0]
    reduced = restrict(fine_rows).reshape(capacity, -1)
    parent = jnp.where(fine_ids >= 0, parent_of[jnp.clip(fine_ids, 0, parent_of.shape[0] - 1)], -1)
    wanted = jnp.arange(lax.axis_size("level") * PAR_DEV, dtype=jnp.int32)
    one_hot = (wanted[:, None] == parent[None, :]).astype(jnp.float32)
    level_sums = lax.psum_scatter(
        jnp.dot(one_hot, reduced, precision=lax.Precision.HIGHEST),
        "level",
        scatter_dimension=0,
        tiled=True,
    )
    group_sums = lax.psum(level_sums, "bal")
    return group_sums.reshape(PAR_DEV, VARS, -1)


def per_device(patches, patch_ids, live, counts, parent_of):
    capacity = patches.shape[0]
    group = lax.axis_size("bal")
    rounds = group.bit_length() - 1
    slot_index = jnp.arange(capacity, dtype=jnp.int32)
    held_count = live[0]
    is_kept = slot_index < held_count
    fine_rows = jnp.where(is_kept[:, None, None], patches, 0.0)
    fine_ids = jnp.where(is_kept, patch_ids, -1)
    coarse = parent_sums(fine_rows, fine_ids, parent_of)
    fine_rows, fine_ids = pairwise_move(fine_rows, fine_ids, held_count, counts, rounds)
    return (fine_rows, fine_ids, coarse)


def solution(mesh):
    return jax.shard_map(
        per_device,
        mesh=mesh,
        in_specs=(
            P(("level", "bal"), None, None),
            P(("level", "bal")),
            P(("level", "bal")),
            P(None, ("level", "bal")),
            P(),
        ),
        out_specs=(P(("level", "bal"), None, None), P(("level", "bal")), P("level", None, None)),
        check_vma=False,
    )
```

profile of v0, /device:TPU:0, one launch (start us, length us, event | category | flops | bytes accessed | tf_op | source)
XLA Modules:
  0.0 143.0 jit_solution(11142344460428278387)
XLA Ops:
  7.2 0.0 copy-start
  7.2 0.0 all-reduce.3.cloned.1.call-start
  7.2 1.3 fusion.13
  9.2 0.6 iota_compare_fusion.5
  10.4 0.0 copy-start.1
  10.4 2.7 %copy_select_fusion = f32[20,5,4096]{2,1,0:T(8,128)S(1)} fusion(f32[20,5,4096]{2,0,1:T(8,128)} %param.5, pred[20]{0:T(512)(128)(4,1)S(1)} %iota_compare_fusion.4), kind=kLoop, calls=%fused_computation.7 | loop fusion | flops 409600 | bytes 3276820 | tf_op jit(solution)/shard_map/jit(_where)/select_n | solution.py:87
  13.1 0.6 gather_fusion.1
  13.7 0.9 broadcast_select_fusion.1
  14.6 0.5 collective-permute-start.1
  15.1 0.0 copy-done.1
  15.1 0.6 gather_fusion
  15.7 0.6 select_convert_fusion.1
  16.3 0.1 collective-permute-start
  16.4 6.2 %copy.14 = f32[20,5,4096]{0,2,1:T(8,128)} copy(f32[20,5,4096]{2,1,0:T(8,128)S(1)} %copy_select_fusion) | data formatting | bytes 3276800 | tf_op jit(solution)/shard_map/jit(_where)/select_n | solution.py:87
  22.6 0.6 iota_compare_fusion.2
  23.3 10.6 %reduce_sum.19 = f32[20,5,8,8,8]{0,4,3,2,1:T(8,128)S(1)} reduce(f32[20,5,8,2,8,2,8,2]{0,7,6,5,4,3,2,1:T(2,128)} %bitcast.30, f32[]{:T(128)} %constant.3.clone.1), dimensions={3,5,7}, to_apply=%region_1.2 | reduce | flops 358400 | bytes 1843204 | tf_op jit(solution)/shard_map/reduce_sum | solution.py:20
  33.9 0.0 copy-start.2
  33.9 0.2 broadcast_multiply_fusion
  34.1 0.0 copy-done
  34.1 0.7 gather_fusion.6
  34.7 0.0 copy-done.2
  34.7 0.6 dynamic-slice
  36.0 0.0 collective-permute-done
  36.0 0.6 fusion.6
  38.0 0.7 fusion.12
  38.7 2.5 %compare_select_fusion.11 = (s32[20]{0:T(128)S(1)}, s32[20]{0:T(128)S(1)}) fusion(s32[20]{0:T(128)S(1)} %gather_fusion.6, s32[20]{0:T(128)S(1)} %get-tuple-element.10, s32[]{:T(128)} %bitcast.10, s32[]{:T(128)} %bitcast.9, s32[]{:T(128)} %bitcast.8, s32[]{:T(128)} %bitcast.7, s32[]{:T(128)S(6)} %sub.42), kind=kLoop, calls=%fused_computation.32 | loop fusion | flops 400 | bytes 340 | tf_op jit(solution)/shard_map/jit(_where)/select_n | solution.py:67
  41.2 0.6 gather_fusion.5
  41.8 0.7 select_convert_fusion
  42.5 3.0 %collective-permute-start.3 = (f32[4]{0:T(128)S(1)}, f32[4]{0:T(128)S(1)}, u32[]{:S(2)}, u32[]{:S(2)}) collective-permute-start(f32[4]{0:T(128)S(1)} %select_convert_fusion), channel_id=1, source_target_pairs={{0,2},{1,3},{2,0},{3,1},{4,6},{5,7},{6,4},{7,5},{8,10},{9,11},{10,... | collective-permute-start | bytes 56 | tf_op jit(solution)/shard_map/ppermute | solution.py:13
  45.5 1.4 fusion
  46.9 0.0 all-reduce.3.cloned.1.call-update
  46.9 0.1 collective-permute-done.3
  47.0 0.7 fusion.11
  47.7 3.0 %fusion.5 = s32[20]{0:T(128)} fusion(s32[20]{0:T(128)S(1)} %get-tuple-element.12, s32[]{:T(128)} %bitcast.11, s32[]{:T(128)} %bitcast.12, s32[]{:T(128)} %bitcast.13, s32[]{:T(128)} %bitcast.14, s32[]{:T(128)S(6)} %sub.43), kind=kLoop, calls=%fused_computation.39 | loop fusion | flops 360 | bytes 180 | tf_op jit(solution)/shard_map/jit(_where)/select_n | solution.py:48
  50.7 0.0 collective-permute-done.1
  50.7 2.2 %gather_fusion.2 = f32[20,5,4096]{2,1,0:T(8,128)} fusion(f32[4,5,4096]{2,1,0:T(8,128)S(1)} %collective-permute-done.1, s32[1024]{0:T(1024)S(1)} %pad_clamp_fusion.3), kind=kCustom, calls=%fused_computation.2 | custom fusion | bytes 3276880 | tf_op jit(solution)/shard_map/gather | solution.py:46
  52.9 3.8 %select_select_fusion.1 = f32[20,5,4096]{2,1,0:T(8,128)S(1)} fusion(f32[20,5,4096]{2,1,0:T(8,128)} %gather_fusion.2, pred[20]{0:T(512)(128)(4,1)S(1)} %get-tuple-element.23, pred[20]{0:T(512)(128)(4,1)S(1)} %get-tuple-element.24, f32[20,5,4096]{2,0,1:T(8,128)} %param.5, pred[20]{0:T(512)(128)(4,1)S(1)} %iota_compare_fusion.4), kind=kLoop, calls=%fused_computation.9 | loop fusion | flops 1228800 | bytes 4915260 | tf_op jit(solution)/shard_map/jit(_where)/select_n | solution.py:43
  56.8 0.6 gather_fusion.3
  57.3 0.9 broadcast_select_fusion
  58.2 2.0 %collective-permute-start.2 = (f32[4,5,4096]{2,1,0:T(8,128)}, f32[4,5,4096]{2,1,0:T(8,128)S(1)}, u32[]{:S(2)}, u32[]{:S(2)}) collective-permute-start(f32[4,5,4096]{2,1,0:T(8,128)} %broadcast_select_fusion), channel_id=1, source_target_pairs={{0,2},{1,3},{2,0},{3,1},{4,6},{5,7},{6,4},{7,5},{8,10},{9,11},{10,... | collective-permute-start | bytes 983048 | tf_op jit(solution)/shard_map/ppermute | solution.py:13
  60.3 57.1 %all-reduce.3.cloned.1.call-done = f32[16,2560]{1,0:T(8,128)} async-done(((f32[16,2560]{1,0:T(8,128)}), f32[16,2560]{1,0:T(8,128)}) %all-reduce.3.cloned.1.call-update) | async-done | bytes 163856
  117.4 0.9 constant_dynamic-slice_fusion
  118.3 10.3 %psum.7 = f32[2,5,512]{2,1,0:T(8,128)S(1)} all-reduce(f32[2,5,512]{2,1,0:T(8,128)S(1)} %reshape.127), channel_id=1, replica_groups=mesh['level'=8,'bal'=4] {'bal'}, use_global_device_ids=true, to_apply=%region_3.4 | all-reduce | flops 5120 | bytes 40960 | tf_op jit(solution)/shard_map/psum | solution.py:76
  128.6 0.6 copy.16
  129.2 0.0 collective-permute-done.2
  129.2 2.2 %gather_fusion.4 = f32[20,5,4096]{2,1,0:T(8,128)} fusion(f32[4,5,4096]{2,1,0:T(8,128)S(1)} %collective-permute-done.2, s32[1024]{0:T(1024)S(1)} %pad_clamp_fusion.1), kind=kCustom, calls=%fused_computation.4 | custom fusion | bytes 3276880 | tf_op jit(solution)/shard_map/gather | solution.py:46
  131.5 2.4 %select_select_fusion = f32[20,5,4096]{2,1,0:T(8,128)S(1)} fusion(f32[20,5,4096]{2,1,0:T(8,128)S(1)} %select_select_fusion.1, f32[20,5,4096]{2,1,0:T(8,128)} %gather_fusion.4, pred[20]{0:T(512)(128)(4,1)S(1)} %get-tuple-element.25, pred[20]{0:T(512)(128)(4,1)S(1)} %get-tuple-element.26), kind=kLoop, calls=%fused_computation.8 | loop fusion | flops 819200 | bytes 4915240 | tf_op jit(solution)/shard_map/jit(_where)/select_n | solution.py:43
  133.9 2.2 %copy.15 = f32[20,5,4096]{2,0,1:T(8,128)} copy(f32[20,5,4096]{2,1,0:T(8,128)S(1)} %select_select_fusion) | data formatting | bytes 3276800
  (16 shorter events, 0.1 us)
Async XLA Ops:
  7.2 26.9 %copy-start = (s32[640]{0:T(1024)S(1)}, s32[640]{0:T(1024)}, u32[]{:S(2)}) copy-start(s32[640]{0:T(1024)} %param.9) | copy-start | bytes 7684
  7.2 110.2 %all-reduce.3.cloned.1.call-start = ((), (), s32[]{:S(2)}) async-start(), calls=%async_computation | async-start | bytes 327680
  10.4 4.7 %copy-start.1 = (s32[20]{0:T(128)S(1)}, s32[20]{0:T(128)}, u32[]{:S(2)}) copy-start(s32[20]{0:T(128)} %param.6) | copy-start | bytes 244
  14.6 36.1 %collective-permute-start.1 = (f32[4,5,4096]{2,1,0:T(8,128)}, f32[4,5,4096]{2,1,0:T(8,128)S(1)}, u32[]{:S(2)}, u32[]{:S(2)}) collective-permute-start(f32[4,5,4096]{2,1,0:T(8,128)} %broadcast_select_fusion.1), channel_id=1, source_target_pairs={{0,1},{1,0},{2,3},{3,2},{4,5},{5,4},{6,7},{7,6},{8,9},{9,8},{10,11... | collective-permute-start | bytes 983048 | tf_op jit(solution)/shard_map/ppermute | solution.py:13
  16.3 19.7 %collective-permute-start = (f32[4]{0:T(128)S(1)}, f32[4]{0:T(128)S(1)}, u32[]{:S(2)}, u32[]{:S(2)}) collective-permute-start(f32[4]{0:T(128)S(1)} %select_convert_fusion.1), channel_id=1, source_target_pairs={{0,1},{1,0},{2,3},{3,2},{4,5},{5,4},{6,7},{7,6},{8,9},{9,8},{10,11... | collective-permute-start | bytes 56 | tf_op jit(solution)/shard_map/ppermute | solution.py:13
  33.9 0.9 copy-start.2
  42.5 4.6 %collective-permute-start.3 = (f32[4]{0:T(128)S(1)}, f32[4]{0:T(128)S(1)}, u32[]{:S(2)}, u32[]{:S(2)}) collective-permute-start(f32[4]{0:T(128)S(1)} %select_convert_fusion), channel_id=1, source_target_pairs={{0,2},{1,3},{2,0},{3,1},{4,6},{5,7},{6,4},{7,5},{8,10},{9,11},{10,... | collective-permute-start | bytes 56 | tf_op jit(solution)/shard_map/ppermute | solution.py:13
  58.2 71.0 %collective-permute-start.2 = (f32[4,5,4096]{2,1,0:T(8,128)}, f32[4,5,4096]{2,1,0:T(8,128)S(1)}, u32[]{:S(2)}, u32[]{:S(2)}) collective-permute-start(f32[4,5,4096]{2,1,0:T(8,128)} %broadcast_select_fusion), channel_id=1, source_target_pairs={{0,2},{1,3},{2,0},{3,1},{4,6},{5,7},{6,4},{7,5},{8,10},{9,11},{10,... | collective-permute-start | bytes 983048 | tf_op jit(solution)/shard_map/ppermute | solution.py:13
Sparse Core Ops, SparseCore 0:
  47.0 70.3 all-reduce.2
where the time goes:
time: 144 us; the launch traced here: 143 us
  waiting for transfers between devices  57.3 us (40%)
  other arithmetic  30.1 us (21%)
  local copies, waits for them, and re-layouts  20.8 us (14%)
  between operations  17.4 us (12%)
  blocking collectives  10.3 us (7%)
  starting transfers between devices  5.65 us (4%)
    unnamed x2, waiting for transfers between devices  57.2 us
    reduce_sum x1, other arithmetic, restrict(): jnp.mean(blocks, axis=(-5, -3, -1))  10.6 us
    psum x1, blocking collectives, parent_sums(): group_sums = lax.psum(level_sums, 'bal')  10.3 us
    select_n x2, other arithmetic, place_rows(): jnp.where(is_kept[:, None, None], fine_rows, jnp.where(is_hit[:, None, No...  6.28 us
    select_n x1, local copies, waits for them, and re-layouts, per_device(): fine_rows = jnp.where(is_kept[:, None, None], patches, 0.0)  6.24 us
    ppermute x4, starting transfers between devices, from_partner(): lax.ppermute(array, axis, [(i, i ^ 1 << stride) for i in range(lax.axis_s...  5.62 us
    gather x2, local copies, waits for them, and re-layouts, place_rows(): in_rows[place_index]  4.45 us
    unnamed x10, local copies, waits for them, and re-layouts  4.34 us
  transfers between devices with their start and end apart: 5, of which 2 were waited for; matrix products, arithmetic and copies ran while one was open for 28% of the time, Pallas kernels for 0%

commit v1 on v0

--- a/solution.py
+++ b/solution.py
@@ -73,7 +73,16 @@
         scatter_dimension=0,
         tiled=True,
     )
-    group_sums = lax.psum(level_sums, "bal")
+    group_sums, piece_next = (level_sums, 0)
+    p_count = lax.axis_size("bal")
+    while 1 << piece_next < p_count:
+        then = lax.ppermute(
+            group_sums,
+            axis_name="bal",
+            perm=[(nth, nth ^ 1 << piece_next) for nth in range(p_count)],
+        )
+        group_sums = group_sums + then
+        piece_next = piece_next + 1
     return group_sums.reshape(PAR_DEV, VARS, -1)
 
 

time: 144 us -> 154 us (1.069)
  waiting for transfers between devices: 57.3 us -> 76.8 us
  blocking collectives: 10.3 us -> 0 us
    psum x1 -> x0, blocking collectives: 10.3 us -> none  [parent_sums(): group_sums = lax.psum(level_sums, 'bal')]
    unnamed x2, waiting for transfers between devices: 57.2 us -> 66.4 us
    ppermute x0 -> x2, waiting for transfers between devices: none -> 8.85 us  [parent_sums(): lax.ppermute(group_sums, axis_name='bal', perm=[(nth, nth ^ 1 << piece_ne...]
    unnamed x10 -> x7, local copies, waits for them, and re-layouts: 4.34 us -> 3.71 us
  transfers between devices with their start and end apart: 5 -> 7, of which waited for: 2 -> 3; matrix products, arithmetic and copies ran while one was open for 28% -> 28% of each run, Pallas kernels for 0% -> 0%
where the time goes in v1:
time: 154 us; the launch traced here: 153 us
  waiting for transfers between devices  76.8 us (50%)
  other arithmetic  31.5 us (20%)
  local copies, waits for them, and re-layouts  20.1 us (13%)
  between operations  17.5 us (11%)
  starting transfers between devices  5.87 us (4%)
    unnamed x2, waiting for transfers between devices  66.4 us
    reduce_sum x1, other arithmetic, restrict(): jnp.mean(blocks, axis=(-5, -3, -1))  10.6 us
    ppermute x2, waiting for transfers between devices, parent_sums(): lax.ppermute(group_sums, axis_name='bal', perm=[(nth, nth ^ 1 << piece_ne...  8.85 us
    select_n x1, local copies, waits for them, and re-layouts, per_device(): fine_rows = jnp.where(is_kept[:, None, None], patches, 0.0)  6.25 us
    select_n x2, other arithmetic, place_rows(): jnp.where(is_kept[:, None, None], fine_rows, jnp.where(is_hit[:, None, No...  6.12 us
    ppermute x4, starting transfers between devices, from_partner(): lax.ppermute(array, axis, [(i, i ^ 1 << stride) for i in range(lax.axis_s...  5.17 us
    gather x2, local copies, waits for them, and re-layouts, place_rows(): in_rows[place_index]  4.45 us
    unnamed x7, local copies, waits for them, and re-layouts  3.71 us
  transfers between devices with their start and end apart: 7, of which 3 were waited for; matrix products, arithmetic and copies ran while one was open for 28% of the time, Pallas kernels for 0%

profile of v1, /device:TPU:0, one launch (start us, length us, event | category | flops | bytes accessed | tf_op | source)
XLA Modules:
  0.0 153.2 jit_solution(4822100619434258024)
XLA Ops:
  7.2 0.0 copy-start
  7.2 0.0 all-reduce.3.cloned.1.call-start
  7.2 1.3 fusion.13
  9.9 0.7 compare_select_fusion
  10.5 0.6 gather_fusion
  11.2 0.7 select_convert_fusion.1
  11.8 0.6 collective-permute-start
  12.4 0.6 iota_compare_fusion.5
  13.1 2.7 %copy_select_fusion = f32[20,5,4096]{2,1,0:T(8,128)S(1)} fusion(f32[20,5,4096]{2,0,1:T(8,128)} %param.5, pred[20]{0:T(512)(128)(4,1)S(1)} %iota_compare_fusion.4), kind=kLoop, calls=%fused_computation.7 | loop fusion | flops 409600 | bytes 3276820 | tf_op jit(solution)/shard_map/jit(_where)/select_n | solution.py:96
  15.8 0.6 gather_fusion.1
  16.3 0.9 broadcast_select_fusion.1
  17.3 0.0 collective-permute-start.1
  17.3 6.2 %copy.14 = f32[20,5,4096]{0,2,1:T(8,128)} copy(f32[20,5,4096]{2,1,0:T(8,128)S(1)} %copy_select_fusion) | data formatting | bytes 3276800 | tf_op jit(solution)/shard_map/jit(_where)/select_n | solution.py:96
  23.6 10.6 %reduce_sum.19 = f32[20,5,8,8,8]{0,4,3,2,1:T(8,128)S(1)} reduce(f32[20,5,8,2,8,2,8,2]{0,7,6,5,4,3,2,1:T(2,128)} %bitcast.31, f32[]{:T(128)} %constant.3.clone.1), dimensions={3,5,7}, to_apply=%region_1.2 | reduce | flops 358400 | bytes 1843204 | tf_op jit(solution)/shard_map/reduce_sum | solution.py:20
  34.1 0.0 copy-start.1
  34.1 0.2 broadcast_multiply_fusion
  34.3 0.7 iota_compare_fusion.2
  35.0 0.0 copy-done
  35.0 0.7 gather_fusion.6
  35.6 0.0 copy-done.1
  35.7 0.6 dynamic-slice
  36.9 0.0 collective-permute-done
  36.9 0.6 fusion.6
  38.9 0.7 fusion.12
  39.5 2.5 %compare_select_fusion.11 = (s32[20]{0:T(128)S(1)}, s32[20]{0:T(128)S(1)}) fusion(s32[20]{0:T(128)S(1)} %gather_fusion.6, s32[20]{0:T(128)S(1)} %get-tuple-element.13, s32[]{:T(128)} %bitcast.10, s32[]{:T(128)} %bitcast.9, s32[]{:T(128)} %bitcast.8, s32[]{:T(128)} %bitcast.7, s32[]{:T(128)S(6)} %sub.42), kind=kLoop, calls=%fused_computation.32 | loop fusion | flops 400 | bytes 340 | tf_op jit(solution)/shard_map/jit(_where)/select_n | solution.py:67
  42.1 1.4 fusion
  43.5 0.0 all-reduce.3.cloned.1.call-update
  43.5 0.6 gather_fusion.5
  44.2 0.7 select_convert_fusion
  44.8 3.0 %collective-permute-start.3 = (f32[4]{0:T(128)S(1)}, f32[4]{0:T(128)S(1)}, u32[]{:S(2)}, u32[]{:S(2)}) collective-permute-start(f32[4]{0:T(128)S(1)} %select_convert_fusion), channel_id=1, source_target_pairs={{0,2},{1,3},{2,0},{3,1},{4,6},{5,7},{6,4},{7,5},{8,10},{9,11},{10,... | collective-permute-start | bytes 56 | tf_op jit(solution)/shard_map/ppermute | solution.py:13
  47.9 1.5 %collective-permute-done.3 = f32[4]{0:T(128)S(1)} collective-permute-done((f32[4]{0:T(128)S(1)}, f32[4]{0:T(128)S(1)}, u32[]{:S(2)}, u32[]{:S(2)}) %collective-permute-start.3) | collective-permute-done | bytes 48 | tf_op jit(solution)/shard_map/ppermute | solution.py:13
  49.4 0.6 fusion.11
  50.0 66.3 %all-reduce.3.cloned.1.call-done = f32[16,2560]{1,0:T(8,128)} async-done(((f32[16,2560]{1,0:T(8,128)}), f32[16,2560]{1,0:T(8,128)}) %all-reduce.3.cloned.1.call-update) | async-done | bytes 163856
  116.4 0.9 constant_dynamic-slice_fusion
  117.3 0.1 collective-permute-start.4
  117.4 0.0 collective-permute-done.1
  117.4 2.2 %gather_fusion.2 = f32[20,5,4096]{2,1,0:T(8,128)} fusion(f32[4,5,4096]{2,1,0:T(8,128)S(1)} %collective-permute-done.1, s32[1024]{0:T(1024)S(1)} %pad_clamp_fusion.3), kind=kCustom, calls=%fused_computation.2 | custom fusion | bytes 3276880 | tf_op jit(solution)/shard_map/gather | solution.py:46
  119.6 3.8 %select_select_fusion.1 = f32[20,5,4096]{2,1,0:T(8,128)S(1)} fusion(f32[20,5,4096]{2,1,0:T(8,128)} %gather_fusion.2, pred[20]{0:T(512)(128)(4,1)S(1)} %get-tuple-element.26, pred[20]{0:T(512)(128)(4,1)S(1)} %get-tuple-element.27, f32[20,5,4096]{2,0,1:T(8,128)} %param.5, pred[20]{0:T(512)(128)(4,1)S(1)} %iota_compare_fusion.4), kind=kLoop, calls=%fused_computation.9 | loop fusion | flops 1228800 | bytes 4915260 | tf_op jit(solution)/shard_map/jit(_where)/select_n | solution.py:43
  123.4 0.6 gather_fusion.3
  124.0 0.1 broadcast_select_fusion
  124.2 1.6 %collective-permute-start.2 = (f32[4,5,4096]{2,1,0:T(8,128)S(1)}, f32[4,5,4096]{2,1,0:T(8,128)S(1)}, u32[]{:S(2)}, u32[]{:S(2)}) collective-permute-start(f32[4,5,4096]{2,1,0:T(8,128)S(1)} %broadcast_select_fusion), channel_id=1, source_target_pairs={{0,2},{1,3},{2,0},{3,1},{4,6},{5,7},{6,4},{7,5},{8,10},{9,11},{10,... | collective-permute-start | bytes 983048 | tf_op jit(solution)/shard_map/ppermute | solution.py:13
  125.7 0.0 collective-permute-done.4
  125.7 0.9 fusion.15
  126.6 0.6 collective-permute-start.5
  127.2 2.9 %fusion.5 = s32[20]{0:T(128)} fusion(s32[20]{0:T(128)S(1)} %get-tuple-element.15, s32[]{:T(128)} %bitcast.11, s32[]{:T(128)} %bitcast.12, s32[]{:T(128)} %bitcast.13, s32[]{:T(128)} %bitcast.14, s32[]{:T(128)S(6)} %sub.43), kind=kLoop, calls=%fused_computation.39 | loop fusion | flops 360 | bytes 180 | tf_op jit(solution)/shard_map/jit(_where)/select_n | solution.py:48
  130.1 8.8 %collective-permute-done.5 = f32[2,2560]{1,0:T(2,128)S(1)} collective-permute-done((f32[2,2560]{1,0:T(2,128)S(1)}, f32[2,2560]{1,0:T(2,128)S(1)}, u32[]{:S(2)}, u32[]{:S(2)}) %collective-permute-start.5) | collective-permute-done | bytes 20512 | tf_op jit(solution)/shard_map/ppermute | solution.py:79
  139.0 0.6 add.95
  139.6 0.0 collective-permute-done.2
  139.6 2.2 %gather_fusion.4 = f32[20,5,4096]{2,1,0:T(8,128)} fusion(f32[4,5,4096]{2,1,0:T(8,128)S(1)} %collective-permute-done.2, s32[1024]{0:T(1024)S(1)} %pad_clamp_fusion.1), kind=kCustom, calls=%fused_computation.4 | custom fusion | bytes 3276880 | tf_op jit(solution)/shard_map/gather | solution.py:46
  141.8 2.3 %select_select_fusion = f32[20,5,4096]{2,1,0:T(8,128)S(1)} fusion(f32[20,5,4096]{2,1,0:T(8,128)S(1)} %select_select_fusion.1, f32[20,5,4096]{2,1,0:T(8,128)} %gather_fusion.4, pred[20]{0:T(512)(128)(4,1)S(1)} %get-tuple-element.28, pred[20]{0:T(512)(128)(4,1)S(1)} %get-tuple-element.29), kind=kLoop, calls=%fused_computation.8 | loop fusion | flops 819200 | bytes 4915240 | tf_op jit(solution)/shard_map/jit(_where)/select_n | solution.py:43
  144.1 2.2 %copy.15 = f32[20,5,4096]{2,0,1:T(8,128)} copy(f32[20,5,4096]{2,1,0:T(8,128)S(1)} %select_select_fusion) | data formatting | bytes 3276800
  (14 shorter events, 0.1 us)
Async XLA Ops:
  7.2 27.8 %copy-start = (s32[640]{0:T(1024)S(1)}, s32[640]{0:T(1024)}, u32[]{:S(2)}) copy-start(s32[640]{0:T(1024)} %param.9) | copy-start | bytes 7684
  7.2 109.2 %all-reduce.3.cloned.1.call-start = ((), (), s32[]{:S(2)}) async-start(), calls=%async_computation | async-start | bytes 327680
  11.8 25.1 %collective-permute-start = (f32[4]{0:T(128)S(1)}, f32[4]{0:T(128)S(1)}, u32[]{:S(2)}, u32[]{:S(2)}) collective-permute-start(f32[4]{0:T(128)S(1)} %select_convert_fusion.1), channel_id=1, source_target_pairs={{0,1},{1,0},{2,3},{3,2},{4,5},{5,4},{6,7},{7,6},{8,9},{9,8},{10,11... | collective-permute-start | bytes 56 | tf_op jit(solution)/shard_map/ppermute | solution.py:13
  17.3 100.1 %collective-permute-start.1 = (f32[4,5,4096]{2,1,0:T(8,128)}, f32[4,5,4096]{2,1,0:T(8,128)S(1)}, u32[]{:S(2)}, u32[]{:S(2)}) collective-permute-start(f32[4,5,4096]{2,1,0:T(8,128)} %broadcast_select_fusion.1), channel_id=1, source_target_pairs={{0,1},{1,0},{2,3},{3,2},{4,5},{5,4},{6,7},{7,6},{8,9},{9,8},{10,11... | collective-permute-start | bytes 983048 | tf_op jit(solution)/shard_map/ppermute | solution.py:13
  34.1 1.5 copy-start.1
  44.8 4.6 %collective-permute-start.3 = (f32[4]{0:T(128)S(1)}, f32[4]{0:T(128)S(1)}, u32[]{:S(2)}, u32[]{:S(2)}) collective-permute-start(f32[4]{0:T(128)S(1)} %select_convert_fusion), channel_id=1, source_target_pairs={{0,2},{1,3},{2,0},{3,1},{4,6},{5,7},{6,4},{7,5},{8,10},{9,11},{10,... | collective-permute-start | bytes 56 | tf_op jit(solution)/shard_map/ppermute | solution.py:13
  117.3 8.4 %collective-permute-start.4 = (f32[2,2560]{1,0:T(2,128)S(1)}, f32[2,2560]{1,0:T(2,128)S(1)}, u32[]{:S(2)}, u32[]{:S(2)}) collective-permute-start(f32[2,2560]{1,0:T(2,128)S(1)} %constant_dynamic-slice_fusion), channel_id=1, source_target_pairs={{0,1},{1,0},{2,3},{3,2},{4,5},{5,4},{6,7},{7,6},{8,9},{9,8},{10,11... | collective-permute-start | bytes 61448 | tf_op jit(solution)/shard_map/ppermute | solution.py:79
  124.2 15.4 %collective-permute-start.2 = (f32[4,5,4096]{2,1,0:T(8,128)S(1)}, f32[4,5,4096]{2,1,0:T(8,128)S(1)}, u32[]{:S(2)}, u32[]{:S(2)}) collective-permute-start(f32[4,5,4096]{2,1,0:T(8,128)S(1)} %broadcast_select_fusion), channel_id=1, source_target_pairs={{0,2},{1,3},{2,0},{3,1},{4,6},{5,7},{6,4},{7,5},{8,10},{9,11},{10,... | collective-permute-start | bytes 983048 | tf_op jit(solution)/shard_map/ppermute | solution.py:13
  126.6 12.3 %collective-permute-start.5 = (f32[2,2560]{1,0:T(2,128)S(1)}, f32[2,2560]{1,0:T(2,128)S(1)}, u32[]{:S(2)}, u32[]{:S(2)}) collective-permute-start(f32[2,2560]{1,0:T(2,128)S(1)} %fusion.15), channel_id=1, source_target_pairs={{0,2},{1,3},{2,0},{3,1},{4,6},{5,7},{6,4},{7,5},{8,10},{9,11},{10,... | collective-permute-start | bytes 61448 | tf_op jit(solution)/shard_map/ppermute | solution.py:79
Sparse Core Ops, SparseCore 0:
  43.6 72.7 all-reduce.2
